TPU v7x, 256 devices: a whole 4x4x8 slice. The times are simulated.
256 devices in a mesh: section: 8 (over x, core), seq: 32 (over z, y).
Axes of the slice: x: 4, y: 4, z: 8, core: 2. Of those that a mesh axis runs over, the one named last changes fastest.
Arguments:
- activations: bfloat16 [8, 8192, 1536], P('section', 'seq'), may hold values from -6 to 6
- qkv_weight: bfloat16 [8, 1536, 4608], P('section'), may hold values from -5 to 5
- out_weight: bfloat16 [8, 1536, 1536], P('section'), may hold values from -0.15625 to 0.15625
- modulation: float32 [8, 3, 1536], P('section'), may hold values from -4 to 4
- key_blocks: int32 [64, 4], replicated, may hold values from 0 to 63, as said below
- block_counts: int32 [64], replicated, may hold values from 3 to 4, as said below
Outputs:
- advanced: bfloat16 [8, 8192, 1536], P('section', 'seq')
Inputs may be any that keep to these rules, and one draw needn't show every extreme that they name: Block b belongs to group b // 2. Row b of key_blocks names first its own block, then the other blocks of its group, then 2 blocks of different groups g with 1 <= |g - b // 2| <= 2. All rows of one group name at most one block of any other group. `block_counts`: some query block uses all 4 entries.
All inputs are finite; a program needn't handle non-finite values.
Results may differ from a plain program's by a relative error of at most 0.008.
Values may be sent and summed in bfloat16 or wider, within the bound.
A program may use at most 128 MiB of HBM per device.

v0:
```python
import jax
import jax.numpy as jnp
from jax import lax
from jax.sharding import PartitionSpec as P

HEADS = 12
HD = 128
BLK = 128


EPSILON = 1e-06


def from_behind(value, axis, steps):
    count = lax.axis_size(axis)
    first, last = (max(0, -steps), min(count, count - steps))
    return lax.ppermute(value, axis, [(source, source + steps) for source in range(first, last)])


def shifted(block, axis, distance):
    devices = range(lax.axis_size(axis))
    route = [((i - distance) % len(devices), i) for i in devices]
    return lax.ppermute(block, axis, route)


def modulated_norm(tokens_in, segment_mod):
    values = tokens_in.astype(jnp.float32)
    center = jnp.mean(values, axis=-1, keepdims=True)
    spread = jnp.mean(jnp.square(values - center), axis=-1, keepdims=True)
    normed = (values - center) * lax.rsqrt(spread + EPSILON)
    return (normed * (1.0 + segment_mod[1]) + segment_mod[0]).astype(jnp.bfloat16)


def owner_tables(key_blocks, seq_count, blocks_here):
    grouped = key_blocks.reshape(seq_count, blocks_here * key_blocks.shape[1])
    owners = grouped // blocks_here
    device_range = jnp.arange(seq_count, dtype=jnp.int32)
    matches = owners[:, :, None] == device_range[None, None, :]
    chosen = jnp.max(jnp.where(matches, (grouped % blocks_here)[:, :, None], 0), axis=1)
    listed = jnp.any(matches, axis=1)
    return (chosen, listed)


def source_id(source, own_chosen, own_listed, seq_count, blocks_here):
    inside = (source >= 0) & (source < seq_count)
    safe = jnp.clip(source, 0, seq_count - 1)
    return jnp.where(inside & own_listed[safe], safe * blocks_here + own_chosen[safe], -1)


def fetch_blocks(local_blocks, key_blocks, own_index):
    seq_count = lax.axis_size("seq")
    blocks_here = local_blocks.shape[0]
    chosen, listed = owner_tables(key_blocks, seq_count, blocks_here)
    own_chosen = lax.dynamic_index_in_dim(chosen, own_index, 0, keepdims=False)
    own_listed = lax.dynamic_index_in_dim(listed, own_index, 0, keepdims=False)
    asked_of_me = lax.dynamic_index_in_dim(chosen, own_index, 1, keepdims=False)
    arrived = []
    arrived_ids = []
    for distance in (1, -1, 2, -2):
        target = jnp.clip(own_index + distance, 0, seq_count - 1)
        incoming = from_behind(
            lax.dynamic_index_in_dim(local_blocks, asked_of_me[target], 0, keepdims=False),
            "seq",
            distance,
        )
        arrived.append(incoming)
        arrived_ids.append(
            source_id(own_index - distance, own_chosen, own_listed, seq_count, blocks_here)
        )
    own_ids = own_index * blocks_here + jnp.arange(blocks_here, dtype=jnp.int32)
    store = jnp.concatenate([local_blocks, jnp.stack(arrived)], axis=0)
    store_ids = jnp.concatenate([own_ids, jnp.stack(arrived_ids)])
    return (store, store_ids)


def attention_output(tokens_in, weights_in, segment_mod, key_blocks, block_counts, own_index):
    token_count = tokens_in.shape[0]
    inner_width = HEADS * HD
    blocks_here = token_count // BLK
    list_width = key_blocks.shape[1]
    modulated = modulated_norm(tokens_in, segment_mod)
    projected = jnp.dot(modulated, weights_in, preferred_element_type=jnp.float32).astype(
        jnp.bfloat16
    )
    queries = projected[:, :inner_width].reshape(blocks_here, BLK, HEADS, HD)
    local_blocks = projected[:, inner_width:].reshape(blocks_here, BLK, 2 * inner_width)
    store, store_ids = fetch_blocks(local_blocks, key_blocks, own_index)
    rows_here = lax.dynamic_slice_in_dim(key_blocks, own_index * blocks_here, blocks_here, 0)
    counts_here = lax.dynamic_slice_in_dim(block_counts, own_index * blocks_here, blocks_here, 0)
    slot_range = jnp.arange(store_ids.shape[0], dtype=jnp.int32)
    slots = jnp.sum(
        jnp.where(rows_here[:, :, None] == store_ids[None, None, :], slot_range[None, None, :], 0),
        axis=-1,
    )
    picked = jnp.take(store, slots.reshape(-1), axis=0).reshape(
        blocks_here, list_width * BLK, 2 * inner_width
    )
    key_part = picked[:, :, :inner_width].reshape(blocks_here, list_width * BLK, HEADS, HD)
    value_part = picked[:, :, inner_width:].reshape(blocks_here, list_width * BLK, HEADS, HD)
    scores = jnp.einsum(
        "bqhd,bkhd->bhqk", queries, key_part, preferred_element_type=jnp.float32
    ) * HD ** (-0.5)
    live = jnp.repeat(
        jnp.arange(list_width, dtype=jnp.int32)[None, :] < counts_here[:, None], BLK, axis=1
    )
    scores = jnp.where(live[:, None, None, :], scores, -jnp.inf)
    row_peak = jnp.max(scores, axis=-1, keepdims=True)
    exponent = jnp.exp(scores - row_peak)
    denominator = jnp.sum(exponent, axis=-1, keepdims=True)
    weighted = jnp.einsum(
        "bhqk,bkhd->bqhd",
        exponent.astype(jnp.bfloat16),
        value_part,
        preferred_element_type=jnp.float32,
    )
    attended = weighted / jnp.moveaxis(denominator, 1, 2)
    return attended.reshape(token_count, inner_width).astype(jnp.bfloat16)


def finish(tokens_in, attended, weights_out, gate_row):
    output = jnp.dot(attended, weights_out, preferred_element_type=jnp.float32)
    return (tokens_in.astype(jnp.float32) + gate_row * output).astype(jnp.bfloat16)


def on_device(activations, qkv_weight, out_weight, modulation, key_blocks, block_counts):
    own_index = lax.axis_index("seq")
    tokens_in = activations[0]
    weights_in = qkv_weight[0]
    weights_out = out_weight[0]
    segment_mod = modulation[0]
    attended = attention_output(
        tokens_in, weights_in, segment_mod, key_blocks, block_counts, own_index
    )
    handed_over = shifted(finish(tokens_in, attended, weights_out, segment_mod[2]), "section", 1)
    second_attended = attention_output(
        handed_over, weights_in, segment_mod, key_blocks, block_counts, own_index
    )
    return finish(handed_over, second_attended, weights_out, segment_mod[2])[None]


def solution(mesh):
    return jax.shard_map(
        on_device,
        mesh=mesh,
        in_specs=(
            P("section", "seq", None),
            P("section", None, None),
            P("section", None, None),
            P("section", None, None),
            P(),
            P(),
        ),
        out_specs=P("section", "seq", None),
        check_vma=False,
    )
```

profile of v0, /device:TPU:120, one launch (start us, length us, event | category | flops | bytes accessed | tf_op | source)
XLA Modules:
  0.0 248.7 jit_solution(9908354819563863701)
XLA Ops:
  0.0 0.8 copy.37
  0.9 0.2 select_reduce_fusion
  1.0 0.7 fusion.100
  6.7 1.3 convert_reduce_fusion.1
  8.1 1.5 fusion.61
  9.6 0.8 slice_reduce_fusion.1
  10.3 9.2 %fusion.4 = bf16[256,4608]{1,0:T(8,128)(2,1)S(1)} fusion(bf16[1,1536,4608]{2,1,0:T(8,128)(2,1)} %param.9, bf16[1,256,1536]{2,1,0:T(8,128)(2,1)} %param.8, f32[1536]{0:T(1024)S(1)} %get-tuple-element.7, f32[1536]{0:T(1024)S(1)} %get-tuple-element.8, f32[256]{0:T(256)S(1)} %add_rsqrt_fusion.1, f32[256]{0:T(256)S(1)} %broadcast_multiply_fusion.1), kind=kOutput, calls=%fused_computation.6 | convolution fusion | flops 3627417600 | bytes 17315840 | tf_op jit(solution)/shard_map/dot_general | solution.py:82
  19.6 1.4 copy-done
  21.0 0.2 slice.54
  23.8 1.7 dynamic-slice_bitcast_fusion.4
  25.5 3.1 %collective-permute-start.3 = (bf16[128,3072]{1,0:T(8,128)(2,1)}, bf16[128,3072]{1,0:T(8,128)(2,1)S(1)}, u32[]{:S(2)}, u32[]{:S(2)}) collective-permute-start(bf16[128,3072]{1,0:T(8,128)(2,1)} %get-tuple-element.17), channel_id=1, source_target_pairs={{2,0},{3,1},{4,2},{5,3},{6,4},{7,5},{8,6},{9,7},{10,8},{11,9},{12,... | collective-permute-start | bytes 2359304 | tf_op jit(solution)/shard_map/ppermute | solution.py:17
  28.7 6.3 %collective-permute-start.2 = (bf16[128,3072]{1,0:T(8,128)(2,1)}, bf16[128,3072]{1,0:T(8,128)(2,1)}, u32[]{:S(2)}, u32[]{:S(2)}) collective-permute-start(bf16[128,3072]{1,0:T(8,128)(2,1)} %get-tuple-element.18), channel_id=1, source_target_pairs={{0,2},{1,3},{2,4},{3,5},{4,6},{5,7},{6,8},{7,9},{8,10},{9,11},{10,... | collective-permute-start | bytes 2359304 | tf_op jit(solution)/shard_map/ppermute | solution.py:17
  35.0 2.7 %collective-permute-start.1 = (bf16[128,3072]{1,0:T(8,128)(2,1)}, bf16[128,3072]{1,0:T(8,128)(2,1)}, u32[]{:S(2)}, u32[]{:S(2)}) collective-permute-start(bf16[128,3072]{1,0:T(8,128)(2,1)} %get-tuple-element.19), channel_id=1, source_target_pairs={{1,0},{2,1},{3,2},{4,3},{5,4},{6,5},{7,6},{8,7},{9,8},{10,9},{11,1... | collective-permute-start | bytes 2359304 | tf_op jit(solution)/shard_map/ppermute | solution.py:17
  37.6 6.7 %collective-permute-start = (bf16[128,3072]{1,0:T(8,128)(2,1)}, bf16[128,3072]{1,0:T(8,128)(2,1)}, u32[]{:S(2)}, u32[]{:S(2)}) collective-permute-start(bf16[128,3072]{1,0:T(8,128)(2,1)} %get-tuple-element.20), channel_id=1, source_target_pairs={{0,1},{1,2},{2,3},{3,4},{4,5},{5,6},{6,7},{7,8},{8,9},{9,10},{10,1... | collective-permute-start | bytes 2359304 | tf_op jit(solution)/shard_map/ppermute | solution.py:17
  44.9 0.6 fusion.101
  50.6 0.2 select_reduce_fusion.1
  50.9 1.5 reshape.225
  52.4 1.2 constant_dynamic-update-slice_fusion
  53.7 36.3 %collective-permute-done = bf16[128,3072]{1,0:T(8,128)(2,1)} collective-permute-done((bf16[128,3072]{1,0:T(8,128)(2,1)}, bf16[128,3072]{1,0:T(8,128)(2,1)}, u32[]{:S(2)}, u32[]{:S(2)}) %collective-permute-start) | collective-permute-done | bytes 786464 | tf_op jit(solution)/shard_map/ppermute | solution.py:17
  90.0 2.1 bitcast_dynamic-update-slice_fusion.7
  92.1 2.2 bitcast_dynamic-update-slice_fusion.6
  94.3 2.1 bitcast_dynamic-update-slice_fusion.5
  96.4 1.0 bitcast_dynamic-update-slice_fusion.4
  97.3 5.9 %gather_fusion = bf16[8,128,3072]{2,1,0:T(8,128)(2,1)} fusion(bf16[6,128,3072]{2,1,0:T(8,128)(2,1)} %bitcast_dynamic-update-slice_fusion.4, s32[1024]{0:T(1024)S(1)} %pad_clamp_fusion), kind=kCustom, calls=%fused_computation.clone | custom fusion | bytes 12582944 | tf_op jit(solution)/shard_map/jit(_take)/gather | solution.py:95
  103.2 3.5 %broadcast_select_fusion.1 = bf16[8,128,3072]{2,1,0:T(8,128)(2,1)S(1)} fusion(bf16[8,128,3072]{2,1,0:T(8,128)(2,1)} %gather_fusion, pred[8]{0:T(512)(128)(4,1)S(1)} %compare_and_fusion), kind=kLoop, calls=%fused_computation.13 | loop fusion | flops 3145728 | bytes 12582920 | tf_op jit(solution)/shard_map/jit(_take)/select_n | solution.py:95
  106.7 3.2 %fusion.99 = (bf16[2,512,1536]{2,1,0:T(8,128)(2,1)}, bf16[2,512,1536]{2,1,0:T(8,128)(2,1)}) fusion(bf16[2,512,3072]{2,1,0:T(8,128)(2,1)S(1)} %bitcast.141), kind=kLoop, calls=%fused_computation.130 | loop fusion | bytes 12582912 | tf_op jit(solution)/shard_map/slice | solution.py:98
  109.9 3.2 %copy.40 = bf16[2,512,1536]{1,2,0:T(8,128)(2,1)S(1)} copy(bf16[2,512,1536]{2,1,0:T(8,128)(2,1)} %get-tuple-element.11) | data formatting | bytes 6291456 | tf_op jit(solution)/shard_map/slice | solution.py:98
  113.1 4.7 %copy.38 = bf16[2,512,1536]{1,2,0:T(8,128)(2,1)} copy(bf16[2,512,1536]{2,1,0:T(8,128)(2,1)} %get-tuple-element.12) | data formatting | bytes 6291456 | tf_op jit(solution)/shard_map/slice | solution.py:99
  117.7 2.4 fusion.10
  120.2 1.7 fusion.12
  121.8 0.2 copy-done.2
  122.0 1.9 fusion.67
  124.0 0.8 copy.43
  124.8 1.4 fusion.44
  126.3 12.6 %collective-permute-done.4 = bf16[256,1536]{1,0:T(8,128)(2,1)S(1)} collective-permute-done((bf16[256,1536]{1,0:T(8,128)(2,1)S(1)}, bf16[256,1536]{1,0:T(8,128)(2,1)S(1)}, u32[]{:S(2)}, u32[]{:S(2)}) %collective-permute-start.4) | collective-permute-done | bytes 786464 | tf_op jit(solution)/shard_map/ppermute | solution.py:23
  138.9 0.2 convert_reduce_fusion
  139.1 0.3 fusion.56
  139.5 4.5 %fusion.7 = bf16[256,4608]{1,0:T(8,128)(2,1)S(1)} fusion(bf16[1,1536,4608]{2,1,0:T(8,128)(2,1)S(1)} %bitcast.161, bf16[256,1536]{1,0:T(8,128)(2,1)S(1)} %collective-permute-done.4, f32[1536]{0:T(1024)S(1)} %get-tuple-element.7, f32[1536]{0:T(1024)S(1)} %get-tuple-element.8, f32[256]{0:T(256)S(1)} %add_rsqrt_fusion, f32[256]{0:T(256)S(1)} %broadcast_multiply_fusion), kind=kOutput, calls=%fused_computation.7 | convolution fusion | flops 3627417600 | bytes 17315840 | tf_op jit(solution)/shard_map/dot_general | solution.py:82
  144.0 0.2 slice.58
  144.2 1.5 dynamic-slice_bitcast_fusion
  145.7 12.2 %collective-permute-start.5 = (bf16[128,3072]{1,0:T(8,128)(2,1)}, bf16[128,3072]{1,0:T(8,128)(2,1)S(1)}, u32[]{:S(2)}, u32[]{:S(2)}) collective-permute-start(bf16[128,3072]{1,0:T(8,128)(2,1)} %get-tuple-element.16), channel_id=1, source_target_pairs={{0,1},{1,2},{2,3},{3,4},{4,5},{5,6},{6,7},{7,8},{8,9},{9,10},{10,1... | collective-permute-start | bytes 2359304 | tf_op jit(solution)/shard_map/ppermute | solution.py:17
  157.9 1.9 collective-permute-start.6
  159.8 1.2 constant_dynamic-update-slice_fusion.1
  161.1 1.5 reshape.226
  162.6 2.6 %collective-permute-start.8 = (bf16[128,3072]{1,0:T(8,128)(2,1)S(1)}, bf16[128,3072]{1,0:T(8,128)(2,1)S(1)}, u32[]{:S(2)}, u32[]{:S(2)}) collective-permute-start(bf16[128,3072]{1,0:T(8,128)(2,1)S(1)} %get-tuple-element.13), channel_id=1, source_target_pairs={{2,0},{3,1},{4,2},{5,3},{6,4},{7,5},{8,6},{9,7},{10,8},{11,9},{12,... | collective-permute-start | bytes 2359304 | tf_op jit(solution)/shard_map/ppermute | solution.py:17
  165.2 7.1 %collective-permute-start.7 = (bf16[128,3072]{1,0:T(8,128)(2,1)}, bf16[128,3072]{1,0:T(8,128)(2,1)S(1)}, u32[]{:S(2)}, u32[]{:S(2)}) collective-permute-start(bf16[128,3072]{1,0:T(8,128)(2,1)} %get-tuple-element.14), channel_id=1, source_target_pairs={{0,2},{1,3},{2,4},{3,5},{4,6},{5,7},{6,8},{7,9},{8,10},{9,11},{10,... | collective-permute-start | bytes 2359304 | tf_op jit(solution)/shard_map/ppermute | solution.py:17
  172.3 4.9 %collective-permute-done.5 = bf16[128,3072]{1,0:T(8,128)(2,1)S(1)} collective-permute-done((bf16[128,3072]{1,0:T(8,128)(2,1)}, bf16[128,3072]{1,0:T(8,128)(2,1)S(1)}, u32[]{:S(2)}, u32[]{:S(2)}) %collective-permute-start.5) | collective-permute-done | bytes 786464 | tf_op jit(solution)/shard_map/ppermute | solution.py:17
  177.2 1.0 bitcast_dynamic-update-slice_fusion.3
  178.2 13.8 %collective-permute-done.6 = bf16[128,3072]{1,0:T(8,128)(2,1)S(1)} collective-permute-done((bf16[128,3072]{1,0:T(8,128)(2,1)}, bf16[128,3072]{1,0:T(8,128)(2,1)S(1)}, u32[]{:S(2)}, u32[]{:S(2)}) %collective-permute-start.6) | collective-permute-done | bytes 786464 | tf_op jit(solution)/shard_map/ppermute | solution.py:17
  192.0 1.0 bitcast_dynamic-update-slice_fusion.2
  193.0 24.1 %collective-permute-done.7 = bf16[128,3072]{1,0:T(8,128)(2,1)S(1)} collective-permute-done((bf16[128,3072]{1,0:T(8,128)(2,1)}, bf16[128,3072]{1,0:T(8,128)(2,1)S(1)}, u32[]{:S(2)}, u32[]{:S(2)}) %collective-permute-start.7) | collective-permute-done | bytes 786464 | tf_op jit(solution)/shard_map/ppermute | solution.py:17
  217.1 0.9 bitcast_dynamic-update-slice_fusion.1
  218.0 1.0 bitcast_dynamic-update-slice_fusion
  219.0 5.9 %gather_fusion.1 = bf16[8,128,3072]{2,1,0:T(8,128)(2,1)} fusion(bf16[6,128,3072]{2,1,0:T(8,128)(2,1)} %bitcast_dynamic-update-slice_fusion, s32[1024]{0:T(1024)S(1)} %pad_clamp_fusion), kind=kCustom, calls=%fused_computation.1.clone | custom fusion | bytes 12582944 | tf_op jit(solution)/shard_map/jit(_take)/gather | solution.py:95
  224.9 3.5 %broadcast_select_fusion = bf16[8,128,3072]{2,1,0:T(8,128)(2,1)S(1)} fusion(bf16[8,128,3072]{2,1,0:T(8,128)(2,1)} %gather_fusion.1, pred[8]{0:T(512)(128)(4,1)S(1)} %compare_and_fusion), kind=kLoop, calls=%fused_computation.12 | loop fusion | flops 3145728 | bytes 12582920 | tf_op jit(solution)/shard_map/jit(_take)/select_n | solution.py:95
  228.3 3.2 %fusion.98 = (bf16[2,512,1536]{2,1,0:T(8,128)(2,1)}, bf16[2,512,1536]{2,1,0:T(8,128)(2,1)}) fusion(bf16[2,512,3072]{2,1,0:T(8,128)(2,1)S(1)} %bitcast.140), kind=kLoop, calls=%fused_computation.129 | loop fusion | bytes 12582912 | tf_op jit(solution)/shard_map/slice | solution.py:98
  231.5 3.2 %copy.46 = bf16[2,512,1536]{1,2,0:T(8,128)(2,1)S(1)} copy(bf16[2,512,1536]{2,1,0:T(8,128)(2,1)} %get-tuple-element.9) | data formatting | bytes 6291456 | tf_op jit(solution)/shard_map/slice | solution.py:98
  234.7 4.7 %copy.44 = bf16[2,512,1536]{1,2,0:T(8,128)(2,1)} copy(bf16[2,512,1536]{2,1,0:T(8,128)(2,1)} %get-tuple-element.10) | data formatting | bytes 6291456 | tf_op jit(solution)/shard_map/slice | solution.py:99
  239.4 2.4 fusion.11
  241.8 1.7 fusion.14
  243.5 0.2 copy-done.1
  243.7 1.9 fusion.66
  245.6 0.8 copy.49
  246.4 2.3 fusion.50
  (59 shorter events, 1.0 us)
Async XLA Ops:
  19.6 1.4 copy-start
  21.0 23.5 %copy-start.6 = (s32[64,4]{0,1:T(4,128)S(1)}, s32[64,4]{0,1:T(4,128)}, u32[]{:S(2)}) copy-start(s32[64,4]{0,1:T(4,128)} %param.12) | copy-start | bytes 3076
  21.0 23.6 %copy-start.7 = (s32[64]{0:T(128)S(1)}, s32[64]{0:T(128)}, u32[]{:S(2)}) copy-start(s32[64]{0:T(128)} %param.13) | copy-start | bytes 772
  21.2 29.7 %slice-start = ((bf16[256,4608]{1,0:T(8,128)(2,1)}), bf16[256,1536]{1,0:T(8,128)(2,1)S(1)}, s32[]{:S(2)}) async-start(bf16[256,4608]{1,0:T(8,128)(2,1)} %copy-done), calls=%async_computation | async-start | bytes 1572864 | tf_op jit(solution)/shard_map/slice | solution.py:85
  25.5 70.8 %collective-permute-start.3 = (bf16[128,3072]{1,0:T(8,128)(2,1)}, bf16[128,3072]{1,0:T(8,128)(2,1)S(1)}, u32[]{:S(2)}, u32[]{:S(2)}) collective-permute-start(bf16[128,3072]{1,0:T(8,128)(2,1)} %get-tuple-element.17), channel_id=1, source_target_pairs={{2,0},{3,1},{4,2},{5,3},{6,4},{7,5},{8,6},{9,7},{10,8},{11,9},{12,... | collective-permute-start | bytes 2359304 | tf_op jit(solution)/shard_map/ppermute | solution.py:17
  28.7 65.6 %collective-permute-start.2 = (bf16[128,3072]{1,0:T(8,128)(2,1)}, bf16[128,3072]{1,0:T(8,128)(2,1)}, u32[]{:S(2)}, u32[]{:S(2)}) collective-permute-start(bf16[128,3072]{1,0:T(8,128)(2,1)} %get-tuple-element.18), channel_id=1, source_target_pairs={{0,2},{1,3},{2,4},{3,5},{4,6},{5,7},{6,8},{7,9},{8,10},{9,11},{10,... | collective-permute-start | bytes 2359304 | tf_op jit(solution)/shard_map/ppermute | solution.py:17
  35.0 57.2 %collective-permute-start.1 = (bf16[128,3072]{1,0:T(8,128)(2,1)}, bf16[128,3072]{1,0:T(8,128)(2,1)}, u32[]{:S(2)}, u32[]{:S(2)}) collective-permute-start(bf16[128,3072]{1,0:T(8,128)(2,1)} %get-tuple-element.19), channel_id=1, source_target_pairs={{1,0},{2,1},{3,2},{4,3},{5,4},{6,5},{7,6},{8,7},{9,8},{10,9},{11,1... | collective-permute-start | bytes 2359304 | tf_op jit(solution)/shard_map/ppermute | solution.py:17
  37.6 52.3 %collective-permute-start = (bf16[128,3072]{1,0:T(8,128)(2,1)}, bf16[128,3072]{1,0:T(8,128)(2,1)}, u32[]{:S(2)}, u32[]{:S(2)}) collective-permute-start(bf16[128,3072]{1,0:T(8,128)(2,1)} %get-tuple-element.20), channel_id=1, source_target_pairs={{0,1},{1,2},{2,3},{3,4},{4,5},{5,6},{6,7},{7,8},{8,9},{9,10},{10,1... | collective-permute-start | bytes 2359304 | tf_op jit(solution)/shard_map/ppermute | solution.py:17
  120.1 1.9 copy-start.2
  120.1 4.7 %slice-start.5 = ((s8[4718592]{0:T(1024)(128)(4,1)}), s8[4194304]{0:T(1024)(128)(4,1)S(1)}, s32[]{:S(2)}) async-start(s8[4718592]{0:T(1024)(128)(4,1)} %bitcast.162), calls=%async_computation.5 | async-start | bytes 8388608
  122.0 2.8 %copy-start.3 = (bf16[1,256,1536]{2,1,0:T(8,128)(2,1)S(1)}, bf16[1,256,1536]{2,1,0:T(8,128)(2,1)}, u32[]{:S(2)}) copy-start(bf16[1,256,1536]{2,1,0:T(8,128)(2,1)} %param.8) | copy-start | bytes 2359300
  122.0 2.8 %slice-start.6 = ((s8[4718592]{0:T(1024)(128)(4,1)}), s8[524288]{0:T(1024)(128)(4,1)S(1)}, s32[]{:S(2)}) async-start(s8[4718592]{0:T(1024)(128)(4,1)} %bitcast.162), calls=%async_computation.6 | async-start | bytes 1048576
  122.0 17.4 %slice-start.1 = ((s8[14155776]{0:T(1024)(128)(4,1)}), s8[1572864]{0:T(1024)(128)(4,1)S(1)}, s32[]{:S(2)}) async-start(s8[14155776]{0:T(1024)(128)(4,1)} %bitcast.160), calls=%async_computation.1 | async-start | bytes 3145728
  122.0 17.4 %slice-start.2 = ((s8[14155776]{0:T(1024)(128)(4,1)}), s8[4194304]{0:T(1024)(128)(4,1)S(1)}, s32[]{:S(2)}) async-start(s8[14155776]{0:T(1024)(128)(4,1)} %bitcast.160), calls=%async_computation.2 | async-start | bytes 8388608
  122.0 17.4 %slice-start.3 = ((s8[14155776]{0:T(1024)(128)(4,1)}), s8[4194304]{0:T(1024)(128)(4,1)S(1)}, s32[]{:S(2)}) async-start(s8[14155776]{0:T(1024)(128)(4,1)} %bitcast.160), calls=%async_computation.3 | async-start | bytes 8388608
  124.8 14.7 %slice-start.4 = ((s8[14155776]{0:T(1024)(128)(4,1)}), s8[4194304]{0:T(1024)(128)(4,1)S(1)}, s32[]{:S(2)}) async-start(s8[14155776]{0:T(1024)(128)(4,1)} %bitcast.160), calls=%async_computation.4 | async-start | bytes 8388608
  126.3 12.6 %collective-permute-start.4 = (bf16[256,1536]{1,0:T(8,128)(2,1)S(1)}, bf16[256,1536]{1,0:T(8,128)(2,1)S(1)}, u32[]{:S(2)}, u32[]{:S(2)}) collective-permute-start(bf16[256,1536]{1,0:T(8,128)(2,1)S(1)} %fusion.44), channel_id=1, source_target_pairs={{224,0},{0,32},{32,64},{64,96},{96,128},{128,160},{160,192},{192,2... | collective-permute-start | bytes 2359304 | tf_op jit(solution)/shard_map/ppermute | solution.py:23
  138.9 5.1 %copy-start.4 = (bf16[256,1536]{1,0:T(8,128)(2,1)}, bf16[256,1536]{1,0:T(8,128)(2,1)S(1)}, u32[]{:S(2)}) copy-start(bf16[256,1536]{1,0:T(8,128)(2,1)S(1)} %collective-permute-done.4) | copy-start | bytes 2359300
  145.7 31.5 %collective-permute-start.5 = (bf16[128,3072]{1,0:T(8,128)(2,1)}, bf16[128,3072]{1,0:T(8,128)(2,1)S(1)}, u32[]{:S(2)}, u32[]{:S(2)}) collective-permute-start(bf16[128,3072]{1,0:T(8,128)(2,1)} %get-tuple-element.16), channel_id=1, source_target_pairs={{0,1},{1,2},{2,3},{3,4},{4,5},{5,6},{6,7},{7,8},{8,9},{9,10},{10,1... | collective-permute-start | bytes 2359304 | tf_op jit(solution)/shard_map/ppermute | solution.py:17
  157.9 34.1 %collective-permute-start.6 = (bf16[128,3072]{1,0:T(8,128)(2,1)}, bf16[128,3072]{1,0:T(8,128)(2,1)S(1)}, u32[]{:S(2)}, u32[]{:S(2)}) collective-permute-start(bf16[128,3072]{1,0:T(8,128)(2,1)} %get-tuple-element.15), channel_id=1, source_target_pairs={{1,0},{2,1},{3,2},{4,3},{5,4},{6,5},{7,6},{8,7},{9,8},{10,9},{11,1... | collective-permute-start | bytes 2359304 | tf_op jit(solution)/shard_map/ppermute | solution.py:17
  162.6 55.4 %collective-permute-start.8 = (bf16[128,3072]{1,0:T(8,128)(2,1)S(1)}, bf16[128,3072]{1,0:T(8,128)(2,1)S(1)}, u32[]{:S(2)}, u32[]{:S(2)}) collective-permute-start(bf16[128,3072]{1,0:T(8,128)(2,1)S(1)} %get-tuple-element.13), channel_id=1, source_target_pairs={{2,0},{3,1},{4,2},{5,3},{6,4},{7,5},{8,6},{9,7},{10,8},{11,9},{12,... | collective-permute-start | bytes 2359304 | tf_op jit(solution)/shard_map/ppermute | solution.py:17
  165.2 51.9 %collective-permute-start.7 = (bf16[128,3072]{1,0:T(8,128)(2,1)}, bf16[128,3072]{1,0:T(8,128)(2,1)S(1)}, u32[]{:S(2)}, u32[]{:S(2)}) collective-permute-start(bf16[128,3072]{1,0:T(8,128)(2,1)} %get-tuple-element.14), channel_id=1, source_target_pairs={{0,2},{1,3},{2,4},{3,5},{4,6},{5,7},{6,8},{7,9},{8,10},{9,11},{10,... | collective-permute-start | bytes 2359304 | tf_op jit(solution)/shard_map/ppermute | solution.py:17
  241.8 1.9 copy-start.1
  241.8 4.6 %slice-start.7 = ((s8[4718592]{0:T(1024)(128)(4,1)}), s8[4194304]{0:T(1024)(128)(4,1)S(1)}, s32[]{:S(2)}) async-start(s8[4718592]{0:T(1024)(128)(4,1)} %bitcast.164), calls=%async_computation.7 | async-start | bytes 8388608
  243.7 2.7 %copy-start.5 = (bf16[256,1536]{1,0:T(8,128)(2,1)S(1)}, bf16[256,1536]{1,0:T(8,128)(2,1)}, u32[]{:S(2)}) copy-start(bf16[256,1536]{1,0:T(8,128)(2,1)} %copy-done.4) | copy-start | bytes 2359300
  243.7 2.7 %slice-start.8 = ((s8[4718592]{0:T(1024)(128)(4,1)}), s8[524288]{0:T(1024)(128)(4,1)S(1)}, s32[]{:S(2)}) async-start(s8[4718592]{0:T(1024)(128)(4,1)} %bitcast.164), calls=%async_computation.8 | async-start | bytes 1048576
where the time goes:
time: 250 us; the launch traced here: 249 us
  waiting for transfers between devices  91.7 us (37%)
  local copies, waits for them, and re-layouts  60.4 us (24%)
  starting transfers between devices  42.6 us (17%)
  matrix products  26 us (10%)
  other arithmetic  15 us (6%)
  between operations  13 us (5%)
    ppermute x8, waiting for transfers between devices, from_behind(): lax.ppermute(value, axis, [(source, source + steps) for source in range(f...  79 us
    ppermute x8, starting transfers between devices, from_behind(): lax.ppermute(value, axis, [(source, source + steps) for source in range(f...  42.6 us
    unnamed x43, local copies, waits for them, and re-layouts  14.5 us
    dot_general x2, matrix products, attention_output(): jnp.dot(modulated, weights_in, preferred_element_type=jnp.float32)  13.7 us
    slice x4, local copies, waits for them, and re-layouts, attention_output(): picked[:, :, :inner_width].reshape(blocks_here, list_width * BLK, HEADS, HD)  12.7 us
    ppermute x1, waiting for transfers between devices, shifted(): return lax.ppermute(block, axis, route)  12.6 us
    gather x2, local copies, waits for them, and re-layouts, attention_output(): jnp.take(store, slots.reshape(-1), axis=0)  11.9 us
    slice x2, local copies, waits for them, and re-layouts, attention_output(): picked[:, :, inner_width:].reshape(blocks_here, list_width * BLK, HEADS, HD)  9.32 us
  transfers between devices with their start and end apart: 9, of which 5 were waited for; matrix products, arithmetic and copies ran while one was open for 7% of the time, Pallas kernels for 0%

commit v1 on v0

v1 whole, which is shorter than its diff:
```python
import functools

import jax
import jax.numpy as jnp
from jax import lax
from jax.experimental import pallas as pl
from jax.experimental.pallas import tpu as pltpu
from jax.sharding import PartitionSpec as P

MESH = pl.DeviceIdType.MESH

D = 1536
HEADS = 12
HD = 128
BLK = 128
EPSILON = 1e-06
NEG = -1e30
SCALE = HD**-0.5 * 1.4426950408889634

CH = 4
ROWS = BLK // CH
TN = 512


def kernel(
    sections,
    seqs,
    kb,
    cnt,
    x_hbm,
    wqkv_hbm,
    wout_hbm,
    mod,
    out_ref,
    xbuf,
    x1,
    xin,
    snd,
    rcv,
    wqkv,
    wout,
    mn,
    mh,
    qb,
    kvo,
    kvh,
    acc,
    mst,
    lst,
    att,
    sem_in,
    send_sem,
    recv_sem,
    shift_send,
    shift_recv,
):
    s = lax.axis_index("section")
    g = lax.axis_index("seq")
    up, down = lax.rem(g + 1, seqs), lax.rem(g + seqs - 1, seqs)
    nxt, prv = lax.rem(s + 1, sections), lax.rem(s + sections - 1, sections)

    x_in = pltpu.make_async_copy(x_hbm, xbuf, sem_in.at[0])
    x_in.start()
    w_in = []
    for j in range(3):
        cols = pl.ds(j * D, D)
        w_in.append(
            pltpu.make_async_copy(wqkv_hbm.at[:, cols], wqkv.at[:, cols], sem_in.at[1 + j])
        )
    w_in.append(pltpu.make_async_copy(wout_hbm, wout, sem_in.at[4]))
    for cp in w_in:
        cp.start()

    barrier = pltpu.get_barrier_semaphore()
    for dev in ((s, up), (s, down), (nxt, g), (prv, g)):
        pl.semaphore_signal(barrier, inc=1, device_id=dev, device_id_type=MESH)

    def wanted(d):
        target = lax.rem(g + d + seqs, seqs)
        pick = jnp.int32(0)
        for r in range(2):
            row = target * 2 + r
            for j in (2, 3):
                entry = kb[row, j]
                live = jnp.logical_and(entry // 2 == g, j < cnt[row])
                pick = jnp.where(live, entry % 2, pick)
        return pick

    picks = [wanted(d) for d in (1, -1, 2, -2)]

    def bias_of(r, d):
        row = g * 2 + r
        hit = jnp.bool_(False)
        for j in (2, 3):
            hit = jnp.logical_or(
                hit, jnp.logical_and(kb[row, j] // 2 == g + d, j < cnt[row])
            )
        return jnp.where(hit, jnp.float32(0.0), jnp.float32(NEG))

    bias = {d: [bias_of(r, d) for r in range(2)] for d in (-1, 1, -2, 2)}

    def flow(l, f, c):
        rows = pl.ds(c * ROWS, ROWS)
        src = snd.at[l, f, rows] if f < 4 else rcv.at[l, f - 2, rows]
        return pltpu.make_async_remote_copy(
            src_ref=src,
            dst_ref=rcv.at[l, f, rows],
            send_sem=send_sem.at[l, f, c],
            recv_sem=recv_sem.at[l, f, c],
            device_id=(s, up if f % 2 == 0 else down),
            device_id_type=MESH,
        )

    def shift(c):
        rows = pl.ds(c * ROWS, ROWS)
        return pltpu.make_async_remote_copy(
            src_ref=x1.at[:, rows],
            dst_ref=xin.at[:, rows],
            send_sem=shift_send.at[c],
            recv_sem=shift_recv.at[c],
            device_id=(nxt, g),
            device_id_type=MESH,
        )

    def normed(v):
        v = v.astype(jnp.float32)
        center = jnp.mean(v, axis=-1, keepdims=True)
        v = v - center
        spread = jnp.mean(jnp.square(v), axis=-1, keepdims=True)
        v = v * lax.rsqrt(spread + EPSILON)
        return (v * (1.0 + mod[1:2, :]) + mod[0:1, :]).astype(jnp.bfloat16)

    NR = 64

    def norm_own(src):
        for r in range(2):

            def body(i, carry):
                rows = pl.ds(pl.multiple_of(i * NR, NR), NR)
                mn[r, rows] = normed(src[r, rows])
                return carry

            lax.fori_loop(0, BLK // NR, body, 0)

    def project(src, w_first, tiles, dst, dst_first, rows_of):
        def body(j, carry):
            wcol = pl.multiple_of(w_first + j * TN, TN)
            dcol = pl.multiple_of(dst_first + j * TN, TN)
            y = jnp.dot(
                src, wqkv[:, pl.ds(wcol, TN)], preferred_element_type=jnp.float32
            ).astype(jnp.bfloat16)
            rows_of(dst, pl.ds(dcol, TN), y)
            return carry

        lax.fori_loop(0, tiles, body, 0)

    def attend(keys, first, last, biases):
        def body(h, carry):
            cols = pl.ds(pl.multiple_of(h * HD, HD), HD)
            vcols = pl.ds(pl.multiple_of(D + h * HD, HD), HD)
            kh = keys(cols)
            vh = keys(vcols)
            for r in range(2):
                qh = qb[r, :, cols]
                sc = lax.dot_general(
                    qh, kh, (((1,), (1,)), ((), ())), preferred_element_type=jnp.float32
                )
                s0 = sc[:, :BLK] * SCALE
                s1 = sc[:, BLK:] * SCALE
                if biases is not None:
                    s0 = s0 + biases[0][r]
                    s1 = s1 + biases[1][r]
                peak = jnp.max(jnp.maximum(s0, s1), axis=-1, keepdims=True)
                if first:
                    mnew = jnp.broadcast_to(peak, (BLK, HD))
                else:
                    mold = mst[h, r]
                    mnew = jnp.maximum(mold, peak)
                p0 = jnp.exp2(s0 - mnew)
                p1 = jnp.exp2(s1 - mnew)
                total = jnp.sum(p0 + p1, axis=-1, keepdims=True)
                p = jnp.concatenate([p0, p1], axis=1).astype(jnp.bfloat16)
                pv = jnp.dot(p, vh, preferred_element_type=jnp.float32)
                if first:
                    lnew = jnp.broadcast_to(total, (BLK, HD))
                else:
                    alpha = jnp.exp2(mold - mnew)
                    lnew = lst[h, r] * alpha + total
                    pv = acc[r, :, cols] * alpha + pv
                if last:
                    att[r, :, cols] = (pv / lnew).astype(jnp.bfloat16)
                else:
                    acc[r, :, cols] = pv
                    mst[h, r] = mnew
                    lst[h, r] = lnew
            return carry

        lax.fori_loop(0, HEADS, body, 0)

    def select(l, src, c):
        rows = pl.ds(c * ROWS, ROWS)
        lower, upper = src[0, rows], src[1, rows]
        for f in range(4):
            snd[l, f, rows] = jnp.where(picks[f] == 0, lower, upper)

    def layer(l, src, emit):
        norm_own(src)
        if l == 0:
            for cp in w_in[:3]:
                cp.wait()

        def put_own(dst, cols, y):
            dst[:, :, cols] = y.reshape(2, BLK, TN)

        own = mn[...].reshape(2 * BLK, D)
        project(own, 0, D // TN, qb, 0, put_own)
        project(own, D, 2 * D // TN, kvo, 0, put_own)
        attend(lambda cols: kvo[:, :, cols].reshape(2 * BLK, HD), True, False, None)

        for c in range(CH):
            for f in (0, 1):
                flow(l, f, c).wait_recv()
        for f in (0, 1):

            def near(i, carry):
                rows = pl.ds(pl.multiple_of(i * NR, NR), NR)
                mh[f, rows] = normed(rcv[l, f, rows])
                return carry

            lax.fori_loop(0, BLK // NR, near, 0)

        def put_near(dst, cols, y):
            dst[0, :, :, cols] = y.reshape(2, BLK, TN)

        project(mh[...].reshape(2 * BLK, D), D, 2 * D // TN, kvh, 0, put_near)
        for c in range(CH // 2):
            for f in (2, 3):
                flow(l, f, c).wait_recv()
                flow(l, f + 2, c).start()
        attend(
            lambda cols: kvh[0, :, :, cols].reshape(2 * BLK, HD),
            False,
            False,
            (bias[-1], bias[1]),
        )
        for c in range(CH // 2, CH):
            for f in (2, 3):
                flow(l, f, c).wait_recv()
                flow(l, f + 2, c).start()

        half = BLK // 2
        for i in range(2):
            rows = pl.ds(i * half, half)
            for c in range(i * CH // 2, (i + 1) * CH // 2):
                for f in (4, 5):
                    flow(l, f, c).wait_recv()
            for f in (4, 5):
                mh[f - 4, rows] = normed(rcv[l, f, rows])

            def put_far(dst, cols, y):
                dst[1, :, rows, cols] = y.reshape(2, half, TN)

            project(mh[:, rows].reshape(2 * half, D), D, 2 * D // TN, kvh, 0, put_far)
        attend(
            lambda cols: kvh[1, :, :, cols].reshape(2 * BLK, HD),
            False,
            True,
            (bias[-2], bias[2]),
        )

        if l == 0:
            w_in[3].wait()
        for i in range(2):
            rows = pl.ds(i * half, half)
            a = att[:, rows].reshape(2 * half, D)
            for j in range(D // TN):
                cols = pl.ds(j * TN, TN)
                y = jnp.dot(a, wout[:, cols], preferred_element_type=jnp.float32)
                res = src[:, rows, cols].astype(jnp.float32).reshape(2 * half, TN)
                res = res + mod[2:3, cols] * y
                emit(rows, cols, res.astype(jnp.bfloat16).reshape(2, half, TN))
            if l == 0:
                for c in range(i * CH // 2, (i + 1) * CH // 2):
                    shift(c).start()

    x_in.wait()
    for c in range(CH):
        select(0, xbuf, c)
    pl.semaphore_wait(barrier, 4)
    for fs in ((0, 1), (2, 3)):
        for c in range(CH):
            for f in fs:
                flow(0, f, c).start()

    def emit_first(rows, cols, y):
        x1[:, rows, cols] = y

    layer(0, xbuf, emit_first)

    for c in range(CH):
        shift(c).wait_recv()
        select(1, xin, c)
        for f in (0, 1):
            flow(1, f, c).start()
    for c in range(CH):
        for f in (2, 3):
            flow(1, f, c).start()

    def emit_second(rows, cols, y):
        out_ref[:, rows, cols] = y

    layer(1, xin, emit_second)

    for c in range(CH):
        shift(c).wait_send()
        for l in range(2):
            for f in range(6):
                flow(l, f, c).wait_send()


def on_device(sections, seqs, activations, qkv_weight, out_weight, modulation, key_blocks, block_counts):
    bf16, f32 = jnp.bfloat16, jnp.float32
    dma = pltpu.SemaphoreType.DMA
    out = pl.pallas_call(
        functools.partial(kernel, sections, seqs),
        out_shape=jax.ShapeDtypeStruct((2, BLK, D), bf16),
        in_specs=[
            pl.BlockSpec(memory_space=pltpu.SMEM),
            pl.BlockSpec(memory_space=pltpu.SMEM),
            pl.BlockSpec(memory_space=pl.ANY),
            pl.BlockSpec(memory_space=pl.ANY),
            pl.BlockSpec(memory_space=pl.ANY),
            pl.BlockSpec(memory_space=pltpu.VMEM),
        ],
        out_specs=pl.BlockSpec(memory_space=pltpu.VMEM),
        scratch_shapes=[
            pltpu.VMEM((2, BLK, D), bf16),
            pltpu.VMEM((2, BLK, D), bf16),
            pltpu.VMEM((2, BLK, D), bf16),
            pltpu.VMEM((2, 4, BLK, D), bf16),
            pltpu.VMEM((2, 6, BLK, D), bf16),
            pltpu.VMEM((D, 3 * D), bf16),
            pltpu.VMEM((D, D), bf16),
            pltpu.VMEM((2, BLK, D), bf16),
            pltpu.VMEM((2, BLK, D), bf16),
            pltpu.VMEM((2, BLK, D), bf16),
            pltpu.VMEM((2, BLK, 2 * D), bf16),
            pltpu.VMEM((2, 2, BLK, 2 * D), bf16),
            pltpu.VMEM((2, BLK, D), f32),
            pltpu.VMEM((HEADS, 2, BLK, HD), f32),
            pltpu.VMEM((HEADS, 2, BLK, HD), f32),
            pltpu.VMEM((2, BLK, D), bf16),
            dma((5,)),
            dma((2, 6, CH)),
            dma((2, 6, CH)),
            dma((CH,)),
            dma((CH,)),
        ],
        compiler_params=pltpu.CompilerParams(
            collective_id=0, has_side_effects=True, vmem_limit_bytes=60 * 1024 * 1024
        ),
        name="two_layers",
    )(
        key_blocks,
        block_counts,
        activations.reshape(2, BLK, D),
        qkv_weight[0],
        out_weight[0],
        modulation[0],
    )
    return out.reshape(1, 2 * BLK, D)


def solution(mesh):
    return jax.shard_map(
        functools.partial(on_device, mesh.shape["section"], mesh.shape["seq"]),
        mesh=mesh,
        in_specs=(
            P("section", "seq", None),
            P("section", None, None),
            P("section", None, None),
            P("section", None, None),
            P(),
            P(),
        ),
        out_specs=P("section", "seq", None),
        check_vma=False,
    )
```

time: 250 us -> 115 us (0.46)
  the two profiles are of different devices: /device:TPU:120 before, /device:TPU:8 now
where the time goes in v1:
time: 115 us
  Pallas kernels  110 us (96%)
  local copies, waits for them, and re-layouts  4.77 us (4%)
    pallas_call x1, Pallas kernels, on_device(): pl.pallas_call(functools.partial(kernel, sections, seqs), out_shape=jax.S...  110 us
    unnamed x3, local copies, waits for them, and re-layouts  4.77 us

profile of v1, /device:TPU:8, one launch (start us, length us, event | category | flops | bytes accessed | tf_op | source)
XLA Modules:
  0.0 115.1 jit_solution(17392240158412189730)
XLA Ops:
  0.0 1.3 %copy.10 = f32[1,3,1536]{2,1,0:T(4,128)} copy(f32[1,3,1536]{2,0,1:T(1,128)} %param.9) | data formatting | bytes 36864
  1.3 1.4 %copy.7.kb = s32[64,4]{1,0:T(8,128)} copy(s32[64,4]{0,1:T(4,128)} %param.10) | data formatting | bytes 2048 | tf_op args[4]
  2.7 110.3 %two_layers.1 = bf16[2,128,1536]{2,1,0:T(8,128)(2,1)} custom-call(s32[64,4]{1,0:T(8,128)} %copy.7.kb, s32[64]{0:T(128)} %cnt.1, bf16[2,128,1536]{2,1,0:T(8,128)(2,1)} %bitcast.10, bf16[1536,4608]{1,0:T(8,128)(2,1)} %bitcast.7, bf16[1536,1536]{1,0:T(8,128)(2,1)} %bitcast.8, f32[3,1536]{1,0:T(4,128)} %bitcast.11), custom_call_target="tpu_custom_call" | custom-call | tf_op jit(solution)/shard_map/two_layers/pallas_call | solution.py:324
  113.0 2.1 %copy.12 = bf16[1,256,1536]{2,1,0:T(8,128)(2,1)} copy(bf16[1,256,1536]{2,1,0:T(8,128)(2,1)} %bitcast.9) | data formatting | bytes 1572864

commit v2 on v1

v2 whole, which is shorter than its diff:
```python
import functools

import jax
import jax.numpy as jnp
from jax import lax
from jax.experimental import pallas as pl
from jax.experimental.pallas import tpu as pltpu
from jax.sharding import PartitionSpec as P

MESH = pl.DeviceIdType.MESH

D = 1536
HEADS = 12
HD = 128
BLK = 128
EPSILON = 1e-06
NEG = -1e30
SCALE = HD**-0.5 * 1.4426950408889634

CH = 4
SH = 8
TN = 512
UH = 4


def kernel(
    sections,
    seqs,
    kb,
    cnt,
    x_hbm,
    wqkv_hbm,
    wout_hbm,
    mod,
    out_ref,
    xbuf,
    x1,
    xin,
    snd,
    rcv,
    wqkv,
    wout,
    mown,
    qkv,
    kvn,
    kvf,
    acc,
    mst,
    lst,
    att,
    sem_in,
    send_sem,
    recv_sem,
    shift_send,
    shift_recv,
):
    s = lax.axis_index("section")
    g = lax.axis_index("seq")
    up, down = lax.rem(g + 1, seqs), lax.rem(g + seqs - 1, seqs)
    nxt, prv = lax.rem(s + 1, sections), lax.rem(s + sections - 1, sections)

    x_in = pltpu.make_async_copy(x_hbm, xbuf, sem_in.at[0])
    x_in.start()
    w_in = []
    for j in range(3):
        cols = pl.ds(j * D, D)
        w_in.append(
            pltpu.make_async_copy(wqkv_hbm.at[:, cols], wqkv.at[:, cols], sem_in.at[1 + j])
        )
    w_in.append(pltpu.make_async_copy(wout_hbm, wout, sem_in.at[4]))
    for cp in w_in:
        cp.start()

    barrier = pltpu.get_barrier_semaphore()
    for dev in ((s, up), (s, down), (nxt, g), (prv, g)):
        pl.semaphore_signal(barrier, inc=1, device_id=dev, device_id_type=MESH)

    def wanted(d):
        target = lax.rem(g + d + seqs, seqs)
        pick = jnp.int32(0)
        for r in range(2):
            row = target * 2 + r
            for j in (2, 3):
                entry = kb[j, row]
                live = jnp.logical_and(entry // 2 == g, j < cnt[row])
                pick = jnp.where(live, entry % 2, pick)
        return pick

    picks = [wanted(d) for d in (1, -1, 2, -2)]

    def bias_of(r, d):
        row = g * 2 + r
        hit = jnp.bool_(False)
        for j in (2, 3):
            hit = jnp.logical_or(
                hit, jnp.logical_and(kb[j, row] // 2 == g + d, j < cnt[row])
            )
        return jnp.where(hit, jnp.float32(0.0), jnp.float32(NEG))

    bias = {d: [bias_of(r, d) for r in range(2)] for d in (-1, 1, -2, 2)}
    lane = lax.broadcasted_iota(jnp.int32, (1, HD), 1)
    far = [jnp.where(lane < BLK // 2, bias[-2][r], bias[2][r]) for r in range(2)]

    def flow(l, f, c, n):
        rows = pl.ds(c * (BLK // n), BLK // n)
        src = snd.at[l, f, rows] if f < 4 else rcv.at[l, f - 2, rows]
        return pltpu.make_async_remote_copy(
            src_ref=src,
            dst_ref=rcv.at[l, f, rows],
            send_sem=send_sem.at[l, f, c],
            recv_sem=recv_sem.at[l, f, c],
            device_id=(s, up if f % 2 == 0 else down),
            device_id_type=MESH,
        )

    def shift(c):
        rows = pl.ds(c * (BLK // SH), BLK // SH)
        return pltpu.make_async_remote_copy(
            src_ref=x1.at[:, rows],
            dst_ref=xin.at[:, rows],
            send_sem=shift_send.at[c],
            recv_sem=shift_recv.at[c],
            device_id=(nxt, g),
            device_id_type=MESH,
        )

    def normed(v):
        v = v.astype(jnp.float32)
        center = jnp.mean(v, axis=-1, keepdims=True)
        v = v - center
        spread = jnp.mean(jnp.square(v), axis=-1, keepdims=True)
        v = v * lax.rsqrt(spread + EPSILON)
        return (v * (1.0 + mod[1]) + mod[0]).astype(jnp.bfloat16)

    def select(l, fs, rows):
        lower, upper = mown[0, rows], mown[1, rows]
        for f in fs:
            snd[l, f, rows] = jnp.where(picks[f] == 0, lower, upper)

    def project(src, w_first, steps, dst):
        def body(j, carry):
            for t in range(D // TN):
                wcol = pl.multiple_of(w_first + j * D + t * TN, TN)
                dcol = pl.multiple_of(j * D + t * TN, TN)
                y = jnp.dot(
                    src(), wqkv[:, pl.ds(wcol, TN)], preferred_element_type=jnp.float32
                )
                dst(pl.ds(dcol, TN), y.astype(jnp.bfloat16))
            return carry

        lax.fori_loop(0, steps, body, 0)

    def attend(keys, first, last):
        def body(i, carry):
            at = []
            for u in range(UH):
                h = i * UH + u
                at.append(pl.ds(pl.multiple_of(h * HD, HD), HD))
            scores, old, new, done = {}, {}, {}, {}
            for u in range(UH):
                h = i * UH + u
                qh = qkv[:, :, at[u]].reshape(2 * BLK, HD)
                if not first:
                    old[u] = (mst[h], lst[h], acc[:, :, at[u]].reshape(2 * BLK, HD))
                parts = []
                for load, masks in keys:
                    sc = lax.dot_general(
                        qh,
                        load(h, 0),
                        (((1,), (1,)), ((), ())),
                        preferred_element_type=jnp.float32,
                    )
                    for k in range(sc.shape[1] // HD):
                        part = sc[:, k * HD : (k + 1) * HD] * SCALE
                        if masks is not None:
                            part = jnp.concatenate(
                                [part[:BLK] + masks[k][0], part[BLK:] + masks[k][1]], axis=0
                            )
                        parts.append(part)
                scores[u] = parts
            for u in range(UH):
                peak = scores[u][0]
                for part in scores[u][1:]:
                    peak = jnp.maximum(peak, part)
                peak = jnp.max(peak, axis=-1, keepdims=True)
                if first:
                    new[u] = jnp.broadcast_to(peak, (2 * BLK, HD))
                else:
                    new[u] = jnp.maximum(old[u][0], peak)
            for u in range(UH):
                ps = [jnp.exp2(part - new[u]) for part in scores[u]]
                total = ps[0]
                for p in ps[1:]:
                    total = total + p
                total = jnp.sum(total, axis=-1, keepdims=True)
                pv, k = None, 0
                for load, _ in keys:
                    v = load(i * UH + u, 1)
                    n = v.shape[0] // HD
                    p = ps[k] if n == 1 else jnp.concatenate(ps[k : k + n], axis=1)
                    k += n
                    y = jnp.dot(
                        p.astype(jnp.bfloat16), v, preferred_element_type=jnp.float32
                    )
                    pv = y if pv is None else pv + y
                if first:
                    total = jnp.broadcast_to(total, (2 * BLK, HD))
                else:
                    alpha = jnp.exp2(old[u][0] - new[u])
                    total = old[u][1] * alpha + total
                    pv = old[u][2] * alpha + pv
                done[u] = (total, pv)
            for u in range(UH):
                total, pv = done[u]
                if last:
                    y = (pv / total).astype(jnp.bfloat16)
                    att[:, :, at[u]] = y.reshape(2, BLK, HD)
                else:
                    h = i * UH + u
                    mst[h] = new[u]
                    lst[h] = total
                    acc[:, :, at[u]] = pv.reshape(2, BLK, HD)
            return carry

        lax.fori_loop(0, HEADS // UH, body, 0)

    def cols_of(h, which, base):
        return pl.ds(pl.multiple_of(base + which * D + h * HD, HD), HD)

    def own_keys(h, which):
        return qkv[:, :, cols_of(h, which, D)].reshape(2 * BLK, HD)

    def near_keys(h, which):
        return kvn[:, :, cols_of(h, which, 0)].reshape(2 * BLK, HD)

    def far_keys(i):
        return lambda h, which: kvf[i, :, cols_of(h, which, 0)]

    def layer(l, src, emit):
        n = CH if l == 0 else SH
        if l == 0:
            x_in.wait()
        for c in range(n):
            rows = pl.ds(c * (BLK // n), BLK // n)
            if l == 1:
                shift(c).wait_recv()
            for r in range(2):
                mown[r, rows] = normed(src[r, rows])
            select(l, (0, 1), rows)
            if l == 0 and c == 0:
                pl.semaphore_wait(barrier, 4)
            for f in (0, 1):
                flow(l, f, c, n).start()
        select(l, (2, 3), pl.ds(0, BLK))
        for c in range(CH):
            for f in (2, 3):
                flow(l, f, c, CH).start()

        if l == 0:
            for cp in w_in[:3]:
                cp.wait()

        def put_own(cols, y):
            qkv[:, :, cols] = y.reshape(2, BLK, TN)

        project(lambda: mown[...].reshape(2 * BLK, D), 0, 3, put_own)

        for c in range(n):
            for f in (0, 1):
                flow(l, f, c, n).wait_recv()

        def put_near(cols, y):
            kvn[:, :, cols] = y.reshape(2, BLK, TN)

        project(lambda: rcv[l, 0:2].reshape(2 * BLK, D), D, 2, put_near)
        for c in range(CH):
            for f in (2, 3):
                flow(l, f, c, CH).wait_recv()
                flow(l, f + 2, c, CH).start()
        attend(
            [(own_keys, None), (near_keys, (bias[-1], bias[1]))],
            True,
            False,
        )

        half = BLK // 2
        for i in range(2):
            rows = pl.ds(i * half, half)
            for c in range(i * CH // 2, (i + 1) * CH // 2):
                for f in (4, 5):
                    flow(l, f, c, CH).wait_recv()

            def put_far(cols, y):
                kvf[i, :, cols] = y

            project(lambda: rcv[l, 4:6, rows].reshape(2 * half, D), D, 2, put_far)
            attend([(far_keys(i), (far,))], False, i == 1)

        if l == 0:
            w_in[3].wait()
        for j in range(D // TN):
            cols = pl.ds(j * TN, TN)
            y = jnp.dot(
                att[...].reshape(2 * BLK, D),
                wout[:, cols],
                preferred_element_type=jnp.float32,
            )
            res = src[:, :, cols].astype(jnp.float32).reshape(2 * BLK, TN)
            res = res + mod[2, :, cols] * y
            emit(cols, res.astype(jnp.bfloat16).reshape(2, BLK, TN))

    def emit_first(cols, y):
        x1[:, :, cols] = y

    def emit_second(cols, y):
        out_ref[:, :, cols] = y

    layer(0, xbuf, emit_first)
    for c in range(SH):
        shift(c).start()
    layer(1, xin, emit_second)

    for c in range(SH):
        shift(c).wait_send()
    for l in range(2):
        for f in range(6):
            n = SH if l == 1 and f < 2 else CH
            for c in range(n):
                flow(l, f, c, n).wait_send()


def on_device(sections, seqs, activations, qkv_weight, out_weight, modulation, key_blocks, block_counts):
    bf16, f32 = jnp.bfloat16, jnp.float32
    dma = pltpu.SemaphoreType.DMA
    out = pl.pallas_call(
        functools.partial(kernel, sections, seqs),
        out_shape=jax.ShapeDtypeStruct((2, BLK, D), bf16),
        in_specs=[
            pl.BlockSpec(memory_space=pltpu.SMEM),
            pl.BlockSpec(memory_space=pltpu.SMEM),
            pl.BlockSpec(memory_space=pltpu.HBM),
            pl.BlockSpec(memory_space=pltpu.HBM),
            pl.BlockSpec(memory_space=pltpu.HBM),
            pl.BlockSpec(memory_space=pltpu.VMEM),
        ],
        out_specs=pl.BlockSpec(memory_space=pltpu.VMEM),
        scratch_shapes=[
            pltpu.VMEM((2, BLK, D), bf16),
            pltpu.VMEM((2, BLK, D), bf16),
            pltpu.VMEM((2, BLK, D), bf16),
            pltpu.VMEM((2, 4, BLK, D), bf16),
            pltpu.VMEM((2, 6, BLK, D), bf16),
            pltpu.VMEM((D, 3 * D), bf16),
            pltpu.VMEM((D, D), bf16),
            pltpu.VMEM((2, BLK, D), bf16),
            pltpu.VMEM((2, BLK, 3 * D), bf16),
            pltpu.VMEM((2, BLK, 2 * D), bf16),
            pltpu.VMEM((2, BLK, 2 * D), bf16),
            pltpu.VMEM((2, BLK, D), f32),
            pltpu.VMEM((HEADS, 2 * BLK, HD), f32),
            pltpu.VMEM((HEADS, 2 * BLK, HD), f32),
            pltpu.VMEM((2, BLK, D), bf16),
            dma((5,)),
            dma((2, 6, SH)),
            dma((2, 6, SH)),
            dma((SH,)),
            dma((SH,)),
        ],
        compiler_params=pltpu.CompilerParams(
            collective_id=0, has_side_effects=True, vmem_limit_bytes=60 * 1024 * 1024
        ),
        name="two_layers",
    )(
        key_blocks.T,
        block_counts,
        activations.reshape(2, BLK, D),
        qkv_weight[0],
        out_weight[0],
        modulation.transpose(1, 0, 2),
    )
    return out.reshape(1, 2 * BLK, D)


def solution(mesh):
    return jax.shard_map(
        functools.partial(on_device, mesh.shape["section"], mesh.shape["seq"]),
        mesh=mesh,
        in_specs=(
            P("section", "seq", None),
            P("section", None, None),
            P("section", None, None),
            P("section", None, None),
            P(),
            P(),
        ),
        out_specs=P("section", "seq", None),
        check_vma=False,
    )
```

time: 115 us -> 82.5 us (0.72)
  the two profiles are of different devices: /device:TPU:8 before, /device:TPU:4 now
where the time goes in v2:
time: 82.5 us; the launch traced here: 82.3 us
  Pallas kernels  80.2 us (97%)
  local copies, waits for them, and re-layouts  2.06 us (2%)
    pallas_call x1, Pallas kernels, on_device(): pl.pallas_call(functools.partial(kernel, sections, seqs), out_shape=jax.S...  80.2 us
    unnamed x1, local copies, waits for them, and re-layouts  2.06 us

profile of v2, /device:TPU:4, one launch (start us, length us, event | category | flops | bytes accessed | tf_op | source)
XLA Modules:
  0.0 82.3 jit_solution(5410167996491979977)
XLA Ops:
  0.0 80.2 %two_layers.1 = bf16[2,128,1536]{2,1,0:T(8,128)(2,1)} custom-call(s32[4,64]{1,0:T(4,128)} %bitcast.11, s32[64]{0:T(128)} %cnt.1, bf16[2,128,1536]{2,1,0:T(8,128)(2,1)} %bitcast.9, bf16[1536,4608]{1,0:T(8,128)(2,1)} %bitcast.6, bf16[1536,1536]{1,0:T(8,128)(2,1)} %bitcast.7, f32[3,1,1536]{2,1,0:T(1,128)} %bitcast.10), custom_call_target="tpu_custom_call" | custom-call | tf_op jit(solution)/shard_map/two_layers/pallas_call | solution.py:335
  80.2 2.1 %copy.8 = bf16[1,256,1536]{2,1,0:T(8,128)(2,1)} copy(bf16[1,256,1536]{2,1,0:T(8,128)(2,1)} %bitcast.8) | data formatting | bytes 1572864

commit v3 on v2

--- a/solution.py
+++ b/solution.py
@@ -21,6 +21,10 @@
 SH = 8
 TN = 512
 UH = 4
+
+
+def aligned(first):
+    return first if isinstance(first, int) else pl.multiple_of(first, HD)
 
 
 def kernel(
@@ -71,9 +75,37 @@
     for cp in w_in:
         cp.start()
 
+    def sends(f):
+        reach = 1 if f < 2 else 2
+        if f < 4:
+            return g + reach < seqs if f % 2 == 0 else g >= reach
+        return interior
+
+    def receives(f):
+        if f < 2:
+            return g >= 1 if f == 0 else g + 1 < seqs
+        if f < 4:
+            return interior
+        return g >= 2 if f == 4 else g + 2 < seqs
+
+    has_up, has_down = g + 1 < seqs, g >= 1
+    interior = jnp.logical_and(has_up, has_down)
+
     barrier = pltpu.get_barrier_semaphore()
-    for dev in ((s, up), (s, down), (nxt, g), (prv, g)):
+    for dev in ((nxt, g), (prv, g)):
         pl.semaphore_signal(barrier, inc=1, device_id=dev, device_id_type=MESH)
+    for dev, there in (((s, up), has_up), ((s, down), has_down)):
+
+        @pl.when(there)
+        def _():
+            pl.semaphore_signal(barrier, inc=1, device_id=dev, device_id_type=MESH)
+
+    for f in (0, 1, 4, 5):
+
+        @pl.when(jnp.logical_not(receives(f)))
+        def _():
+            for l in range(2):
+                rcv[l, f] = jnp.zeros((BLK, D), jnp.bfloat16)
 
     def wanted(d):
         target = lax.rem(g + d + seqs, seqs)
@@ -137,7 +169,7 @@
         for f in fs:
             snd[l, f, rows] = jnp.where(picks[f] == 0, lower, upper)
 
-    def project(src, w_first, steps, dst):
+    def project(src, w_first, steps, dst, scaled=False):
         def body(j, carry):
             for t in range(D // TN):
                 wcol = pl.multiple_of(w_first + j * D + t * TN, TN)
@@ -145,87 +177,90 @@
                 y = jnp.dot(
                     src(), wqkv[:, pl.ds(wcol, TN)], preferred_element_type=jnp.float32
                 )
+                if scaled:
+                    y = y * jnp.where(j == 0, jnp.float32(SCALE), jnp.float32(1.0))
                 dst(pl.ds(dcol, TN), y.astype(jnp.bfloat16))
             return carry
 
         lax.fori_loop(0, steps, body, 0)
 
-    def attend(keys, first, last):
+    def heads(i, keys, first, last):
+        at = []
+        for u in range(UH):
+            h = i * UH + u
+            at.append(pl.ds(aligned(h * HD), HD))
+        scores, old, new, done = {}, {}, {}, {}
+        for u in range(UH):
+            h = i * UH + u
+            qh = qkv[:, :, at[u]].reshape(2 * BLK, HD)
+            if not first:
+                old[u] = (mst[h], lst[h], acc[:, :, at[u]].reshape(2 * BLK, HD))
+            parts = []
+            for load, masks in keys:
+                sc = lax.dot_general(
+                    qh,
+                    load(h, 0),
+                    (((1,), (1,)), ((), ())),
+                    preferred_element_type=jnp.float32,
+                )
+                for k in range(sc.shape[1] // HD):
+                    part = sc[:, k * HD : (k + 1) * HD]
+                    if masks is not None:
+                        part = jnp.concatenate(
+                            [part[:BLK] + masks[k][0], part[BLK:] + masks[k][1]], axis=0
+                        )
+                    parts.append(part)
+            scores[u] = parts
+        for u in range(UH):
+            peak = scores[u][0]
+            for part in scores[u][1:]:
+                peak = jnp.maximum(peak, part)
+            peak = jnp.max(peak, axis=-1, keepdims=True)
+            if first:
+                new[u] = jnp.broadcast_to(peak, (2 * BLK, HD))
+            else:
+                new[u] = jnp.maximum(old[u][0], peak)
+        for u in range(UH):
+            ps = [jnp.exp2(part - new[u]) for part in scores[u]]
+            pv, k = None, 0
+            for load, _ in keys:
+                v = load(i * UH + u, 1)
+                n = v.shape[0] // HD
+                p = ps[k] if n == 1 else jnp.concatenate(ps[k : k + n], axis=1)
+                k += n
+                v = jnp.concatenate([v, jnp.ones_like(v)], axis=1)
+                y = jnp.dot(
+                    p.astype(jnp.bfloat16), v, preferred_element_type=jnp.float32
+                )
+                pv = y if pv is None else pv + y
+            pv, total = pv[:, :HD], pv[:, HD:]
+            if not first:
+                alpha = jnp.exp2(old[u][0] - new[u])
+                total = old[u][1] * alpha + total
+                pv = old[u][2] * alpha + pv
+            done[u] = (total, pv)
+        for u in range(UH):
+            total, pv = done[u]
+            if last:
+                y = (pv / total).astype(jnp.bfloat16)
+                att[:, :, at[u]] = y.reshape(2, BLK, HD)
+            else:
+                h = i * UH + u
+                mst[h] = new[u]
+                lst[h] = total
+                acc[:, :, at[u]] = pv.reshape(2, BLK, HD)
+
+    def attend(keys, first, last, before=None):
         def body(i, carry):
-            at = []
-            for u in range(UH):
-                h = i * UH + u
-                at.append(pl.ds(pl.multiple_of(h * HD, HD), HD))
-            scores, old, new, done = {}, {}, {}, {}
-            for u in range(UH):
-                h = i * UH + u
-                qh = qkv[:, :, at[u]].reshape(2 * BLK, HD)
-                if not first:
-                    old[u] = (mst[h], lst[h], acc[:, :, at[u]].reshape(2 * BLK, HD))
-                parts = []
-                for load, masks in keys:
-                    sc = lax.dot_general(
-                        qh,
-                        load(h, 0),
-                        (((1,), (1,)), ((), ())),
-                        preferred_element_type=jnp.float32,
-                    )
-                    for k in range(sc.shape[1] // HD):
-                        part = sc[:, k * HD : (k + 1) * HD] * SCALE
-                        if masks is not None:
-                            part = jnp.concatenate(
-                                [part[:BLK] + masks[k][0], part[BLK:] + masks[k][1]], axis=0
-                            )
-                        parts.append(part)
-                scores[u] = parts
-            for u in range(UH):
-                peak = scores[u][0]
-                for part in scores[u][1:]:
-                    peak = jnp.maximum(peak, part)
-                peak = jnp.max(peak, axis=-1, keepdims=True)
-                if first:
-                    new[u] = jnp.broadcast_to(peak, (2 * BLK, HD))
-                else:
-                    new[u] = jnp.maximum(old[u][0], peak)
-            for u in range(UH):
-                ps = [jnp.exp2(part - new[u]) for part in scores[u]]
-                total = ps[0]
-                for p in ps[1:]:
-                    total = total + p
-                total = jnp.sum(total, axis=-1, keepdims=True)
-                pv, k = None, 0
-                for load, _ in keys:
-                    v = load(i * UH + u, 1)
-                    n = v.shape[0] // HD
-                    p = ps[k] if n == 1 else jnp.concatenate(ps[k : k + n], axis=1)
-                    k += n
-                    y = jnp.dot(
-                        p.astype(jnp.bfloat16), v, preferred_element_type=jnp.float32
-                    )
-                    pv = y if pv is None else pv + y
-                if first:
-                    total = jnp.broadcast_to(total, (2 * BLK, HD))
-                else:
-                    alpha = jnp.exp2(old[u][0] - new[u])
-                    total = old[u][1] * alpha + total
-                    pv = old[u][2] * alpha + pv
-                done[u] = (total, pv)
-            for u in range(UH):
-                total, pv = done[u]
-                if last:
-                    y = (pv / total).astype(jnp.bfloat16)
-                    att[:, :, at[u]] = y.reshape(2, BLK, HD)
-                else:
-                    h = i * UH + u
-                    mst[h] = new[u]
-                    lst[h] = total
-                    acc[:, :, at[u]] = pv.reshape(2, BLK, HD)
+            if before is not None:
+                before(i)
+            heads(i, keys, first, last)
             return carry
 
         lax.fori_loop(0, HEADS // UH, body, 0)
 
     def cols_of(h, which, base):
-        return pl.ds(pl.multiple_of(base + which * D + h * HD, HD), HD)
+        return pl.ds(aligned(base + which * D + h * HD), HD)
 
     def own_keys(h, which):
         return qkv[:, :, cols_of(h, which, D)].reshape(2 * BLK, HD)
@@ -248,13 +283,22 @@
                 mown[r, rows] = normed(src[r, rows])
             select(l, (0, 1), rows)
             if l == 0 and c == 0:
-                pl.semaphore_wait(barrier, 4)
+                peers = 2 + has_up.astype(jnp.int32) + has_down.astype(jnp.int32)
+                pl.semaphore_wait(barrier, peers)
             for f in (0, 1):
-                flow(l, f, c, n).start()
+
+                @pl.when(sends(f))
+                def _():
+                    flow(l, f, c, n).start()
+
         select(l, (2, 3), pl.ds(0, BLK))
-        for c in range(CH):
-            for f in (2, 3):
-                flow(l, f, c, CH).start()
+        for f in (2, 3):
+
+            @pl.when(sends(f))
+            def _():
+                for c in range(CH):
+                    flow(l, f, c, CH).start()
+
 
         if l == 0:
             for cp in w_in[:3]:
@@ -263,38 +307,55 @@
         def put_own(cols, y):
             qkv[:, :, cols] = y.reshape(2, BLK, TN)
 
-        project(lambda: mown[...].reshape(2 * BLK, D), 0, 3, put_own)
-
-        for c in range(n):
-            for f in (0, 1):
-                flow(l, f, c, n).wait_recv()
+        project(lambda: mown[...].reshape(2 * BLK, D), 0, 3, put_own, True)
+
+        for f in (0, 1):
+
+            @pl.when(receives(f))
+            def _():
+                for c in range(n):
+                    flow(l, f, c, n).wait_recv()
 
         def put_near(cols, y):
             kvn[:, :, cols] = y.reshape(2, BLK, TN)
 
         project(lambda: rcv[l, 0:2].reshape(2 * BLK, D), D, 2, put_near)
-        for c in range(CH):
-            for f in (2, 3):
-                flow(l, f, c, CH).wait_recv()
-                flow(l, f + 2, c, CH).start()
-        attend(
-            [(own_keys, None), (near_keys, (bias[-1], bias[1]))],
-            True,
-            False,
-        )
+
+
+        def relay(c):
+            @pl.when(interior)
+            def _():
+                for f in (2, 3):
+                    flow(l, f, c, CH).wait_recv()
+                    flow(l, f + 2, c, CH).start()
+
+        attend([(own_keys, None), (near_keys, (bias[-1], bias[1]))], True, False, relay)
+        for c in range(HEADS // UH, CH):
+            relay(c)
 
         half = BLK // 2
         for i in range(2):
             rows = pl.ds(i * half, half)
-            for c in range(i * CH // 2, (i + 1) * CH // 2):
-                for f in (4, 5):
-                    flow(l, f, c, CH).wait_recv()
-
-            def put_far(cols, y):
-                kvf[i, :, cols] = y
-
-            project(lambda: rcv[l, 4:6, rows].reshape(2 * half, D), D, 2, put_far)
-            attend([(far_keys(i), (far,))], False, i == 1)
+            for f in (4, 5):
+
+                @pl.when(receives(f))
+                def _():
+                    for c in range(i * CH // 2, (i + 1) * CH // 2):
+                        flow(l, f, c, CH).wait_recv()
+
+            groups = HEADS // UH
+            wide = UH * HD
+            for j in range(groups + 1):
+                if j < groups:
+                    for first in (j * wide, D + j * wide):
+                        y = jnp.dot(
+                            rcv[l, 4:6, rows].reshape(2 * half, D),
+                            wqkv[:, pl.ds(D + first, wide)],
+                            preferred_element_type=jnp.float32,
+                        )
+                        kvf[i, :, pl.ds(first, wide)] = y.astype(jnp.bfloat16)
+                if j >= 1:
+                    heads(j - 1, [(far_keys(i), (far,))], False, i == 1)
 
         if l == 0:
             w_in[3].wait()
@@ -322,11 +383,14 @@
 
     for c in range(SH):
         shift(c).wait_send()
-    for l in range(2):
-        for f in range(6):
-            n = SH if l == 1 and f < 2 else CH
-            for c in range(n):
-                flow(l, f, c, n).wait_send()
+    for f in range(6):
+
+        @pl.when(sends(f))
+        def _():
+            for l in range(2):
+                n = SH if l == 1 and f < 2 else CH
+                for c in range(n):
+                    flow(l, f, c, n).wait_send()
 
 
 def on_device(sections, seqs, activations, qkv_weight, out_weight, modulation, key_blocks, block_counts):
@@ -334,7 +398,7 @@
     dma = pltpu.SemaphoreType.DMA
     out = pl.pallas_call(
         functools.partial(kernel, sections, seqs),
-        out_shape=jax.ShapeDtypeStruct((2, BLK, D), bf16),
+        out_shape=pltpu.VMEM((2, BLK, D), bf16),
         in_specs=[
             pl.BlockSpec(memory_space=pltpu.SMEM),
             pl.BlockSpec(memory_space=pltpu.SMEM),
@@ -367,7 +431,7 @@
             dma((SH,)),
         ],
         compiler_params=pltpu.CompilerParams(
-            collective_id=0, has_side_effects=True, vmem_limit_bytes=60 * 1024 * 1024
+            collective_id=0, has_side_effects=True, vmem_limit_bytes=62 * 1024 * 1024
         ),
         name="two_layers",
     )(

time: 82.5 us -> 73.4 us (0.89)
  the two profiles are of different devices: /device:TPU:4 before, /device:TPU:120 now
where the time goes in v3:
time: 73.4 us; the launch traced here: 73.3 us
  Pallas kernels  72.4 us (99%)
  local copies, waits for them, and re-layouts  0.88 us (1%)
    pallas_call x1, Pallas kernels, on_device(): pl.pallas_call(functools.partial(kernel, sections, seqs), out_shape=pltpu...  72.4 us

profile of v3, /device:TPU:120, one launch (start us, length us, event | category | flops | bytes accessed | tf_op | source)
XLA Modules:
  0.0 73.3 jit_solution(10506666296015162262)
XLA Ops:
  0.0 72.4 %two_layers.1 = bf16[2,128,1536]{2,1,0:T(8,128)(2,1)S(1)} custom-call(s32[4,64]{1,0:T(4,128)} %bitcast.11, s32[64]{0:T(128)} %cnt.1, bf16[2,128,1536]{2,1,0:T(8,128)(2,1)} %bitcast.9, bf16[1536,4608]{1,0:T(8,128)(2,1)} %bitcast.7, bf16[1536,1536]{1,0:T(8,128)(2,1)} %bitcast.8, f32[3,1,1536]{2,1,0:T(1,128)} %bitcast.10), custom_call_target="tpu_custom_call" | custom-call | tf_op jit(solution)/shard_map/two_layers/pallas_call | solution.py:399
  72.4 0.9 %copy.8 = bf16[1,256,1536]{2,1,0:T(8,128)(2,1)} copy(bf16[1,256,1536]{2,1,0:T(8,128)(2,1)S(1)} %bitcast.6) | data formatting | bytes 1572864

commit v4 on v3

--- a/solution.py
+++ b/solution.py
@@ -63,8 +63,13 @@
     up, down = lax.rem(g + 1, seqs), lax.rem(g + seqs - 1, seqs)
     nxt, prv = lax.rem(s + 1, sections), lax.rem(s + sections - 1, sections)
 
-    x_in = pltpu.make_async_copy(x_hbm, xbuf, sem_in.at[0])
-    x_in.start()
+    x_in = []
+    for j, rows in enumerate((pl.ds(0, BLK // CH), pl.ds(BLK // CH, BLK - BLK // CH))):
+        x_in.append(
+            pltpu.make_async_copy(x_hbm.at[:, rows], xbuf.at[:, rows], sem_in.at[5 * j])
+        )
+    for cp in x_in:
+        cp.start()
     w_in = []
     for j in range(3):
         cols = pl.ds(j * D, D)
@@ -99,13 +104,6 @@
         @pl.when(there)
         def _():
             pl.semaphore_signal(barrier, inc=1, device_id=dev, device_id_type=MESH)
-
-    for f in (0, 1, 4, 5):
-
-        @pl.when(jnp.logical_not(receives(f)))
-        def _():
-            for l in range(2):
-                rcv[l, f] = jnp.zeros((BLK, D), jnp.bfloat16)
 
     def wanted(d):
         target = lax.rem(g + d + seqs, seqs)
@@ -129,9 +127,7 @@
             )
         return jnp.where(hit, jnp.float32(0.0), jnp.float32(NEG))
 
-    bias = {d: [bias_of(r, d) for r in range(2)] for d in (-1, 1, -2, 2)}
-    lane = lax.broadcasted_iota(jnp.int32, (1, HD), 1)
-    far = [jnp.where(lane < BLK // 2, bias[-2][r], bias[2][r]) for r in range(2)]
+    bias, far = {}, []
 
     def flow(l, f, c, n):
         rows = pl.ds(c * (BLK // n), BLK // n)
@@ -184,7 +180,7 @@
 
         lax.fori_loop(0, steps, body, 0)
 
-    def heads(i, keys, first, last):
+    def heads(i, keys, first, last, beside=()):
         at = []
         for u in range(UH):
             h = i * UH + u
@@ -211,6 +207,8 @@
                         )
                     parts.append(part)
             scores[u] = parts
+        for work in beside:
+            work()
         for u in range(UH):
             peak = scores[u][0]
             for part in scores[u][1:]:
@@ -220,6 +218,8 @@
                 new[u] = jnp.broadcast_to(peak, (2 * BLK, HD))
             else:
                 new[u] = jnp.maximum(old[u][0], peak)
+        for work in ():
+            work()
         for u in range(UH):
             ps = [jnp.exp2(part - new[u]) for part in scores[u]]
             pv, k = None, 0
@@ -273,10 +273,10 @@
 
     def layer(l, src, emit):
         n = CH if l == 0 else SH
-        if l == 0:
-            x_in.wait()
         for c in range(n):
             rows = pl.ds(c * (BLK // n), BLK // n)
+            if l == 0 and c < 2:
+                x_in[c].wait()
             if l == 1:
                 shift(c).wait_recv()
             for r in range(2):
@@ -301,6 +301,18 @@
 
 
         if l == 0:
+            for f in (0, 1, 4, 5):
+
+                @pl.when(jnp.logical_not(receives(f)))
+                def _():
+                    for l in range(2):
+                        rcv[l, f] = jnp.zeros((BLK, D), jnp.bfloat16)
+
+            for d in (-1, 1, -2, 2):
+                bias[d] = [bias_of(r, d) for r in range(2)]
+            lane = lax.broadcasted_iota(jnp.int32, (1, HD), 1)
+            for r in range(2):
+                far.append(jnp.where(lane < BLK // 2, bias[-2][r], bias[2][r]))
             for cp in w_in[:3]:
                 cp.wait()
 
@@ -345,17 +357,24 @@
 
             groups = HEADS // UH
             wide = UH * HD
-            for j in range(groups + 1):
-                if j < groups:
-                    for first in (j * wide, D + j * wide):
-                        y = jnp.dot(
-                            rcv[l, 4:6, rows].reshape(2 * half, D),
-                            wqkv[:, pl.ds(D + first, wide)],
-                            preferred_element_type=jnp.float32,
-                        )
-                        kvf[i, :, pl.ds(first, wide)] = y.astype(jnp.bfloat16)
-                if j >= 1:
-                    heads(j - 1, [(far_keys(i), (far,))], False, i == 1)
+
+            def keys_of(first):
+                def work():
+                    y = jnp.dot(
+                        rcv[l, 4:6, rows].reshape(2 * half, D),
+                        wqkv[:, pl.ds(D + first, wide)],
+                        preferred_element_type=jnp.float32,
+                    )
+                    kvf[i, :, pl.ds(first, wide)] = y.astype(jnp.bfloat16)
+
+                return work
+
+            pending = [[keys_of(j * wide), keys_of(D + j * wide)] for j in range(groups)]
+            for work in pending[0]:
+                work()
+            for j in range(groups):
+                beside = pending[j + 1] if j + 1 < groups else []
+                heads(j, [(far_keys(i), (far,))], False, i == 1, beside)
 
         if l == 0:
             w_in[3].wait()
@@ -424,7 +443,7 @@
             pltpu.VMEM((HEADS, 2 * BLK, HD), f32),
             pltpu.VMEM((HEADS, 2 * BLK, HD), f32),
             pltpu.VMEM((2, BLK, D), bf16),
-            dma((5,)),
+            dma((6,)),
             dma((2, 6, SH)),
             dma((2, 6, SH)),
             dma((SH,)),

time: 73.4 us -> 72.4 us (0.986)
  Pallas kernels: 72.4 us -> 71.4 us
    pallas_call x1, Pallas kernels: 72.4 us -> 71.4 us  [on_device(): pl.pallas_call(functools.partial(kernel, sections, seqs), out_shape=pltpu...]
where the time goes in v4:
time: 72.4 us; the launch traced here: 72.3 us
  Pallas kernels  71.4 us (99%)
  local copies, waits for them, and re-layouts  0.88 us (1%)
    pallas_call x1, Pallas kernels, on_device(): pl.pallas_call(functools.partial(kernel, sections, seqs), out_shape=pltpu...  71.4 us

profile of v4, /device:TPU:120, one launch (start us, length us, event | category | flops | bytes accessed | tf_op | source)
XLA Modules:
  0.0 72.3 jit_solution(11154185504351635708)
XLA Ops:
  0.0 71.4 %two_layers.1 = bf16[2,128,1536]{2,1,0:T(8,128)(2,1)S(1)} custom-call(s32[4,64]{1,0:T(4,128)} %bitcast.11, s32[64]{0:T(128)} %cnt.1, bf16[2,128,1536]{2,1,0:T(8,128)(2,1)} %bitcast.9, bf16[1536,4608]{1,0:T(8,128)(2,1)} %bitcast.7, bf16[1536,1536]{1,0:T(8,128)(2,1)} %bitcast.8, f32[3,1,1536]{2,1,0:T(1,128)} %bitcast.10), custom_call_target="tpu_custom_call" | custom-call | tf_op jit(solution)/shard_map/two_layers/pallas_call | solution.py:418
  71.4 0.9 %copy.8 = bf16[1,256,1536]{2,1,0:T(8,128)(2,1)} copy(bf16[1,256,1536]{2,1,0:T(8,128)(2,1)S(1)} %bitcast.6) | data formatting | bytes 1572864
